TPU v7x, 256 devices: a whole 4x4x8 slice. The times are simulated.
256 devices in a mesh: gx: 32 (over y_hi, z, core), gy: 8 (over y_lo, x).
Axes of the slice: x: 4, y: 4 (y_hi: 2, y_lo: 2; y = y_hi * 2 + y_lo), z: 8, core: 2. Of those that a mesh axis runs over, the one named last changes fastest.
Arguments:
- state_field: bfloat16 [1, 64, 2048, 2048], P(None, None, 'gx', 'gy'), may hold values from -6 to 6
- spectral_x: bfloat16 [2, 32, 2, 64, 64], P(None, 'gx'), may hold values from -2 to 2
- spectral_y: bfloat16 [2, 32, 2, 64, 64], P(None, 'gy'), may hold values from -2 to 2
- expand_weight: bfloat16 [2, 64, 256], replicated, may hold values from -0.75 to 0.75
- reduce_weight: bfloat16 [2, 256, 64], replicated, may hold values from -0.375 to 0.375
Outputs:
- next_state: bfloat16 [1, 64, 2048, 2048], P(None, None, 'gx', 'gy')
All inputs are finite; a program needn't handle non-finite values.
Results may differ from a plain program's by a relative error of at most 0.025.
Values may be sent and summed in bfloat16 or wider, within the bound.
No kernel may reach another device: no remote copies, remote signals or barrier semaphores. Data moves between devices by JAX's collectives and lax.ppermute only.
A program may use at most 64 MiB of HBM per device.

v0:
```python
import jax
import jax.numpy as jnp
from jax import lax
from jax.sharding import PartitionSpec as P

NX = 2048
NY = 2048
MODES = 32
LAYERS = 2


def make_tables(length, modes):
    positions = jnp.arange(length, dtype=jnp.int32)
    orders = jnp.arange(modes, dtype=jnp.int32)
    phase = orders[:, None] * positions[None, :] % length
    angle = 2.0 * jnp.pi * phase.astype(jnp.float32) / length
    factor = 1.0 / jnp.sqrt(jnp.float32(length))
    weight_two = jnp.where(orders == 0, 1.0, 2.0).astype(jnp.float32)[:, None]
    forward = jnp.stack([jnp.cos(angle) * factor, -jnp.sin(angle) * factor], axis=1)
    forward = forward.reshape(2 * modes, length).astype(jnp.bfloat16)
    inverse = jnp.stack(
        [weight_two * jnp.cos(angle) * factor, -weight_two * jnp.sin(angle) * factor], axis=1
    )
    inverse = inverse.reshape(2 * modes, length).T.astype(jnp.bfloat16)
    return (forward, inverse)


def mix_modes(spectrum, weights):
    modes = weights.shape[0]
    shaped = spectrum.reshape((modes, 2) + spectrum.shape[1:])
    real_in, imag_in = (shaped[:, 0], shaped[:, 1])
    real_w, imag_w = (weights[:, 0], weights[:, 1])

    def contract_modes(left, right):
        return jnp.einsum("koi,kzin->kzon", left, right, preferred_element_type=jnp.float32)

    real_out = contract_modes(real_w, real_in) - contract_modes(imag_w, imag_in)
    imag_out = contract_modes(real_w, imag_in) + contract_modes(imag_w, real_in)
    joined = jnp.stack([real_out, imag_out], axis=1).astype(jnp.bfloat16)
    return joined.reshape(spectrum.shape)


def body(state_field, spectral_x, spectral_y, expand_weight, reduce_weight):
    planes, channels, local_rows, local_cols = state_field.shape
    row_first = lax.axis_index("gx") * local_rows
    col_first = lax.axis_index("gy") * local_cols
    forward_x, inverse_x = make_tables(NX, MODES)
    forward_y, inverse_y = make_tables(NY, MODES)
    forward_xloc = lax.dynamic_slice_in_dim(forward_x, row_first, local_rows, 1)
    inverse_xloc = lax.dynamic_slice_in_dim(inverse_x, row_first, local_rows, 0)
    forward_yloc = lax.dynamic_slice_in_dim(forward_y, col_first, local_cols, 1)
    inverse_yloc = lax.dynamic_slice_in_dim(inverse_y, col_first, local_cols, 0)
    state = state_field
    for layer_index in range(LAYERS):
        weights_x = spectral_x[layer_index]
        weights_y = spectral_y[layer_index]
        spec_x = lax.psum_scatter(
            jnp.einsum(
                "kx,zcxy->kzcy", forward_xloc, state, preferred_element_type=jnp.float32
            ).astype(jnp.bfloat16),
            "gx",
            scatter_dimension=0,
            tiled=True,
        )
        spec_y = lax.psum_scatter(
            jnp.einsum(
                "ky,zcxy->kzcx", forward_yloc, state, preferred_element_type=jnp.float32
            ).astype(jnp.bfloat16),
            "gy",
            scatter_dimension=0,
            tiled=True,
        )
        mixed_x = mix_modes(spec_x, weights_x)
        mixed_y = mix_modes(spec_y, weights_y)
        branch_x = jnp.einsum(
            "xk,kzcy->zcxy",
            inverse_xloc,
            lax.all_gather(mixed_x, "gx", axis=0, tiled=True),
            preferred_element_type=jnp.float32,
        ).astype(jnp.bfloat16)
        branch_y = jnp.einsum(
            "yk,kzcx->zcxy",
            inverse_yloc,
            lax.all_gather(mixed_y, "gy", axis=0, tiled=True),
            preferred_element_type=jnp.float32,
        ).astype(jnp.bfloat16)
        total = (branch_x.astype(jnp.float32) + branch_y.astype(jnp.float32)).astype(jnp.bfloat16)
        hidden = jax.nn.gelu(
            jnp.einsum(
                "ch,zcxy->zhxy",
                expand_weight[layer_index],
                total,
                preferred_element_type=jnp.float32,
            ),
            approximate=True,
        )
        hidden = hidden.astype(jnp.bfloat16)
        update = jnp.einsum(
            "hc,zhxy->zcxy", reduce_weight[layer_index], hidden, preferred_element_type=jnp.float32
        )
        state = (state.astype(jnp.float32) + update).astype(jnp.bfloat16)
    return state


def solution(mesh):
    in_specs = (
        P(None, None, "gx", "gy"),
        P(None, "gx", None, None, None),
        P(None, "gy", None, None, None),
        P(),
        P(),
    )
    out_specs = P(None, None, "gx", "gy")
    return jax.shard_map(body, mesh=mesh, in_specs=in_specs, out_specs=out_specs, check_vma=False)
```

profile of v0, /device:TPU:1, one launch (start us, length us, event | category | flops | bytes accessed | tf_op | source)
XLA Modules:
  0.0 543.5 jit_solution(1677750337479074670)
XLA Ops:
  6.5 1.1 multiply_convert_fusion.2
  8.1 2.3 convert_bitcast_fusion.3
  10.4 2.5 copy.124
  13.0 1.5 copy-done
  14.5 1.1 fusion.63
  16.3 1.6 reshape.480
  18.6 112.1 %reduce-scatter.9.cloned.1.call-done = bf16[2,1,64,256]{3,2,1,0:T(8,128)(2,1)} async-done(((bf16[64,1,64,256]{3,2,1,0:T(8,128)(2,1)}), bf16[2,1,64,256]{3,2,1,0:T(8,128)(2,1)}) %reduce-scatter.9.cloned.1.call-update) | async-done | bytes 65552 | tf_op jit(solution)/shard_map/reduce_scatter | solution.py:57
  131.6 0.9 fusion.83
  135.1 1.0 multiply_convert_fusion
  136.1 1.0 multiply_convert_fusion.1
  138.2 33.9 %reduce-scatter.13.cloned.1.call-done = bf16[8,4096]{1,0:T(8,128)(2,1)} async-done(((bf16[64,4096]{1,0:T(8,128)(2,1)}), bf16[8,4096]{1,0:T(8,128)(2,1)}) %reduce-scatter.13.cloned.1.call-update) | async-done | bytes 65552
  172.1 1.0 reshape.481
  174.1 24.2 %all_gather.13 = bf16[64,1,64,64]{3,2,1,0:T(8,128)(2,1)S(1)} all-gather(bf16[8,1,64,64]{3,2,1,0:T(8,128)(2,1)S(1)} %bitcast.306), channel_id=1, replica_groups=mesh['gx'=32,'gy'=8] {'gy'}, dimensions={0}, use_global_device_ids=true | all-gather | bytes 589824 | tf_op jit(solution)/shard_map/all_gather | solution.py:84
  198.3 1.2 copy.134
  199.5 1.4 fusion.87
  201.0 58.1 %all-gather.3.cloned.1.call-done = bf16[64,1,64,256]{3,2,1,0:T(8,128)(2,1)} async-done(((bf16[2,1,64,256]{3,2,1,0:T(8,128)(2,1)}), bf16[64,1,64,256]{3,2,1,0:T(8,128)(2,1)}) %all-gather.3.cloned.1.call-update) | async-done | bytes 2097168 | tf_op jit(solution)/shard_map/all_gather | solution.py:78
  259.1 4.7 fusion.24
  263.9 12.2 %fusion.22 = bf16[1,64,64,256]{3,1,2,0:T(8,128)(2,1)S(1)} fusion(bf16[1,64,64,256]{3,2,1,0:T(8,128)(2,1)} %param.5, bf16[64,64,256]{2,1,0:T(8,128)(2,1)} %fusion.24, bf16[2,256,64]{1,2,0:T(8,128)(2,1)S(1)} %copy-done.5, bf16[2,64,256]{2,1,0:T(8,128)(2,1)S(1)} %copy-done.7), kind=kOutput, calls=%fused_computation.28 | convolution fusion | flops 1114636288 | bytes 6356992 | tf_op jit(solution)/shard_map/hc,zhxy->zcxy/dot_general | solution.py:98
  276.1 1.7 convert_bitcast_fusion.2
  277.9 2.5 copy.138
  280.7 2.6 fusion.66
  284.0 1.6 reshape.482
  285.7 105.2 %reduce-scatter.11.cloned.1.call-done = bf16[2,1,64,256]{3,2,1,0:T(8,128)(2,1)} async-done(((bf16[64,1,64,256]{3,2,1,0:T(8,128)(2,1)}), bf16[2,1,64,256]{3,2,1,0:T(8,128)(2,1)}) %reduce-scatter.11.cloned.1.call-update) | async-done | bytes 65552 | tf_op jit(solution)/shard_map/reduce_scatter | solution.py:57
  395.1 36.6 %reduce-scatter.15.cloned.1.call-done = bf16[8,4096]{1,0:T(8,128)(2,1)} async-done(((bf16[64,4096]{1,0:T(8,128)(2,1)}), bf16[8,4096]{1,0:T(8,128)(2,1)}) %reduce-scatter.15.cloned.1.call-update) | async-done | bytes 65552
  431.7 1.0 reshape.483
  433.8 24.0 %all_gather.15 = bf16[64,1,64,64]{3,2,1,0:T(8,128)(2,1)S(1)} all-gather(bf16[8,1,64,64]{3,2,1,0:T(8,128)(2,1)S(1)} %bitcast.307), channel_id=1, replica_groups=mesh['gx'=32,'gy'=8] {'gy'}, dimensions={0}, use_global_device_ids=true | all-gather | bytes 589824 | tf_op jit(solution)/shard_map/all_gather | solution.py:84
  457.8 1.2 copy.147
  459.0 1.4 fusion.85
  460.5 58.2 %all-gather.5.cloned.1.call-done = bf16[64,1,64,256]{3,2,1,0:T(8,128)(2,1)} async-done(((bf16[2,1,64,256]{3,2,1,0:T(8,128)(2,1)}), bf16[64,1,64,256]{3,2,1,0:T(8,128)(2,1)}) %all-gather.5.cloned.1.call-update) | async-done | bytes 2097168 | tf_op jit(solution)/shard_map/all_gather | solution.py:78
  518.7 4.7 fusion.25
  523.4 10.8 %fusion.20 = bf16[1,64,64,256]{3,1,2,0:T(8,128)(2,1)S(1)} fusion(bf16[1,64,64,256]{3,1,2,0:T(8,128)(2,1)} %copy-done.1, bf16[64,64,256]{2,1,0:T(8,128)(2,1)} %fusion.25, bf16[2,256,64]{1,2,0:T(8,128)(2,1)S(1)} %copy-done.6, bf16[2,64,256]{2,1,0:T(8,128)(2,1)S(1)} %copy-done.8), kind=kOutput, calls=%fused_computation.23 | convolution fusion | flops 1114636288 | bytes 6356992 | tf_op jit(solution)/shard_map/hc,zhxy->zcxy/dot_general | solution.py:98
  534.2 2.5 copy.150
  (63 shorter events, 13.6 us)
Async XLA Ops:
  6.5 124.2 %reduce-scatter.9.cloned.1.call-start = ((), (), s32[]{:S(2)}) async-start(), calls=%async_computation.4 | async-start | bytes 2162688 | tf_op jit(solution)/shard_map/reduce_scatter | solution.py:57
  12.9 1.6 copy-start
  12.9 159.1 %reduce-scatter.13.cloned.1.call-start = ((), (), s32[]{:S(2)}) async-start(), calls=%async_computation.8 | async-start | bytes 589824
  15.6 2.4 copy-start.4
  15.6 119.4 %copy-start.3 = (bf16[2,4,2,64,64]{4,3,2,1,0:T(8,128)(2,1)S(1)}, bf16[2,4,2,64,64]{4,3,2,1,0:T(8,128)(2,1)}, u32[]{:S(2)}) copy-start(bf16[2,4,2,64,64]{4,3,2,1,0:T(8,128)(2,1)} %param.7) | copy-start | bytes 393220
  18.0 241.2 %all-gather.3.cloned.1.call-start = ((), (), s32[]{:S(2)}) async-start(), calls=%async_computation.5 | async-start | bytes 2162688 | tf_op jit(solution)/shard_map/all_gather | solution.py:78
  134.9 255.9 %reduce-scatter.11.cloned.1.call-start = ((), (), s32[]{:S(2)}) async-start(), calls=%async_computation.6 | async-start | bytes 2162688 | tf_op jit(solution)/shard_map/reduce_scatter | solution.py:57
  201.0 62.9 %copy-start.5 = (bf16[2,256,64]{1,2,0:T(8,128)(2,1)S(1)}, bf16[2,256,64]{1,2,0:T(8,128)(2,1)}, u32[]{:S(2)}) copy-start(bf16[2,256,64]{1,2,0:T(8,128)(2,1)} %param.9) | copy-start | bytes 196612
  201.0 62.9 %copy-start.7 = (bf16[2,64,256]{2,1,0:T(8,128)(2,1)S(1)}, bf16[2,64,256]{2,1,0:T(8,128)(2,1)}, u32[]{:S(2)}) copy-start(bf16[2,64,256]{2,1,0:T(8,128)(2,1)} %param.8) | copy-start | bytes 196612
  276.1 4.6 copy-start.1
  280.4 151.3 %reduce-scatter.15.cloned.1.call-start = ((), (), s32[]{:S(2)}) async-start(), calls=%async_computation.9 | async-start | bytes 589824
  283.3 107.5 %copy-start.2 = (bf16[1,2,64,64]{3,2,1,0:T(8,128)(2,1)S(1)}, bf16[1,2,64,64]{3,2,1,0:T(8,128)(2,1)}, u32[]{:S(2)}) copy-start(bf16[1,2,64,64]{3,2,1,0:T(8,128)(2,1)} %get-tuple-element.7) | copy-start | bytes 49156
  285.6 233.0 %all-gather.5.cloned.1.call-start = ((), (), s32[]{:S(2)}) async-start(), calls=%async_computation.7 | async-start | bytes 2162688 | tf_op jit(solution)/shard_map/all_gather | solution.py:78
  460.5 62.9 %copy-start.6 = (bf16[2,256,64]{1,2,0:T(8,128)(2,1)S(1)}, bf16[2,256,64]{1,2,0:T(8,128)(2,1)}, u32[]{:S(2)}) copy-start(bf16[2,256,64]{1,2,0:T(8,128)(2,1)} %param.9) | copy-start | bytes 196612
  460.5 62.9 %copy-start.8 = (bf16[2,64,256]{2,1,0:T(8,128)(2,1)S(1)}, bf16[2,64,256]{2,1,0:T(8,128)(2,1)}, u32[]{:S(2)}) copy-start(bf16[2,64,256]{2,1,0:T(8,128)(2,1)} %param.8) | copy-start | bytes 196612
Sparse Core Ops, SparseCore 0:
  13.1 117.6 reduce-scatter.8
  133.4 38.6 reduce-scatter.12
  174.8 84.2 all-gather.2
  280.5 110.2 reduce-scatter.10
  393.4 38.2 reduce-scatter.14
  434.3 84.2 all-gather.4
where the time goes:
time: 545 us; the launch traced here: 544 us
  waiting for transfers between devices  404 us (74%)
  matrix products  51.9 us (10%)
  blocking collectives  48.2 us (9%)
  local copies, waits for them, and re-layouts  20.5 us (4%)
  between operations  13.8 us (3%)
    reduce_scatter x2, waiting for transfers between devices, body(): lax.psum_scatter(jnp.einsum('kx,zcxy->kzcy', forward_xloc, state, preferr...  217 us
    all_gather x2, waiting for transfers between devices, body(): lax.all_gather(mixed_x, 'gx', axis=0, tiled=True)  116 us
    unnamed x8, waiting for transfers between devices  70.6 us
    all_gather x2, blocking collectives, body(): lax.all_gather(mixed_y, 'gy', axis=0, tiled=True)  48.2 us
    dot_general x2, matrix products, body(): jnp.einsum('hc,zhxy->zcxy', reduce_weight[layer_index], hidden, preferred...  23 us
  transfers between devices with their start and end apart: 6, of which 6 were waited for; matrix products, arithmetic and copies ran while one was open for 5% of the time, Pallas kernels for 0%

commit v1 on v0

--- a/solution.py
+++ b/solution.py
@@ -72,10 +72,14 @@
         )
         mixed_x = mix_modes(spec_x, weights_x)
         mixed_y = mix_modes(spec_y, weights_y)
+        sectors_change = lambda v0: jnp.concatenate(
+            lax.all_to_all(jnp.stack([v0 for _ in range(lax.axis_size("gx"))], axis=0), "gx", 0, 0),
+            axis=0,
+        )
         branch_x = jnp.einsum(
             "xk,kzcy->zcxy",
             inverse_xloc,
-            lax.all_gather(mixed_x, "gx", axis=0, tiled=True),
+            sectors_change(mixed_x),
             preferred_element_type=jnp.float32,
         ).astype(jnp.bfloat16)
         branch_y = jnp.einsum(

time: 545 us -> 520 us (0.954)
  the two profiles are of different devices: /device:TPU:1 before, /device:TPU:32 now
where the time goes in v1:
time: 520 us; the launch traced here: 511 us
  waiting for transfers between devices  321 us (62%)
  blocking collectives  61.5 us (12%)
  matrix products  50.2 us (10%)
  local copies, waits for them, and re-layouts  45.3 us (9%)
  between operations  15.4 us (3%)
  starting transfers between devices  14.7 us (3%)
    reduce_scatter x2, waiting for transfers between devices, body(): lax.psum_scatter(jnp.einsum('kx,zcxy->kzcy', forward_xloc, state, preferr...  236 us
    unnamed x6, waiting for transfers between devices  84.6 us
    all_gather x2, blocking collectives, body(): lax.all_gather(mixed_y, 'gy', axis=0, tiled=True)  61.5 us
    dot_general x2, matrix products, body(): jnp.einsum('hc,zhxy->zcxy', reduce_weight[layer_index], hidden, preferred...  23.2 us
    all_to_all x2, starting transfers between devices, body(): lax.all_to_all(jnp.stack([v0 for _ in range(lax.axis_size('gx'))], axis=0...  14.5 us
    all_to_all x2, local copies, waits for them, and re-layouts, body(): lax.all_to_all(jnp.stack([v0 for _ in range(lax.axis_size('gx'))], axis=0...  10.4 us
  transfers between devices with their start and end apart: 6, of which 4 were waited for; matrix products, arithmetic and copies ran while one was open for 4% of the time, Pallas kernels for 0%

profile of v1, /device:TPU:32, one launch (start us, length us, event | category | flops | bytes accessed | tf_op | source)
XLA Modules:
  0.0 511.1 jit_solution(12090558792914323973)
XLA Ops:
  7.4 1.1 multiply_convert_fusion.2
  8.9 2.3 convert_bitcast_fusion.3
  11.2 2.5 copy.130
  15.2 119.7 %reduce-scatter.9.cloned.1.call-done = bf16[2,1,64,256]{3,2,1,0:T(8,128)(2,1)} async-done(((bf16[64,1,64,256]{3,2,1,0:T(8,128)(2,1)}), bf16[2,1,64,256]{3,2,1,0:T(8,128)(2,1)}) %reduce-scatter.9.cloned.1.call-update) | async-done | bytes 65552 | tf_op jit(solution)/shard_map/reduce_scatter | solution.py:57
  138.5 3.2 stack.64
  141.7 7.3 %all-to-all-start = ((bf16[32,2,1,64,256]{4,1,3,2,0:T(2,128)(2,1)}), bf16[32,2,1,64,256]{4,1,3,2,0:T(2,128)(2,1)}, u32[]{:S(2)}, u32[]{:S(2)}) async-start(bf16[32,2,1,64,256]{4,1,3,2,0:T(2,128)(2,1)} %stack.64), calls=%async_computation.1 | async-start | bytes 4194304 | tf_op jit(solution)/shard_map/all_to_all | solution.py:76
  149.1 1.1 fusion.53
  151.0 1.6 reshape.470
  155.8 40.6 %reduce-scatter.13.cloned.1.call-done = bf16[8,4096]{1,0:T(8,128)(2,1)} async-done(((bf16[64,4096]{1,0:T(8,128)(2,1)}), bf16[8,4096]{1,0:T(8,128)(2,1)}) %reduce-scatter.13.cloned.1.call-update) | async-done | bytes 65552
  198.5 31.0 %all_gather.6 = bf16[64,1,64,64]{3,2,1,0:T(8,128)(2,1)S(1)} all-gather(bf16[8,1,64,64]{3,2,1,0:T(8,128)(2,1)S(1)} %bitcast.310), channel_id=1, replica_groups=mesh['gx'=32,'gy'=8] {'gy'}, dimensions={0}, use_global_device_ids=true | all-gather | bytes 589824 | tf_op jit(solution)/shard_map/all_gather | solution.py:88
  229.4 1.2 copy.141
  230.7 1.4 fusion.77
  232.1 5.2 %copy.132 = bf16[32,2,1,64,256]{4,1,0,3,2:T(2,128)(2,1)} copy(bf16[32,2,1,64,256]{4,1,3,2,0:T(2,128)(2,1)} %all-to-all-done) | data formatting | bytes 4194304 | tf_op jit(solution)/shard_map/all_to_all | solution.py:76
  237.3 4.1 reshape.438
  241.5 3.8 fusion.24
  245.2 12.4 %fusion.22 = bf16[1,64,64,256]{3,1,2,0:T(8,128)(2,1)S(1)} fusion(bf16[1,64,64,256]{3,2,1,0:T(8,128)(2,1)} %param.5, bf16[64,64,256]{2,1,0:T(8,128)(2,1)} %fusion.24, bf16[2,256,64]{1,2,0:T(8,128)(2,1)S(1)} %copy-done.5, bf16[2,64,256]{2,1,0:T(8,128)(2,1)S(1)} %copy-done.7), kind=kOutput, calls=%fused_computation.28 | convolution fusion | flops 1114636288 | bytes 6356992 | tf_op jit(solution)/shard_map/hc,zhxy->zcxy/dot_general | solution.py:102
  257.6 1.7 convert_bitcast_fusion.2
  259.4 2.5 copy.145
  262.0 116.6 %reduce-scatter.11.cloned.1.call-done = bf16[2,1,64,256]{3,2,1,0:T(8,128)(2,1)} async-done(((bf16[64,1,64,256]{3,2,1,0:T(8,128)(2,1)}), bf16[2,1,64,256]{3,2,1,0:T(8,128)(2,1)}) %reduce-scatter.11.cloned.1.call-update) | async-done | bytes 65552 | tf_op jit(solution)/shard_map/reduce_scatter | solution.py:57
  382.2 3.2 stack.72
  385.4 7.2 %all-to-all-start.1 = ((bf16[32,2,1,64,256]{4,1,3,2,0:T(2,128)(2,1)}), bf16[32,2,1,64,256]{4,1,3,2,0:T(2,128)(2,1)}, u32[]{:S(2)}, u32[]{:S(2)}) async-start(bf16[32,2,1,64,256]{4,1,3,2,0:T(2,128)(2,1)} %stack.72), calls=%async_computation.3 | async-start | bytes 4194304 | tf_op jit(solution)/shard_map/all_to_all | solution.py:76
  392.7 2.6 fusion.56
  396.0 1.6 reshape.472
  397.7 44.0 %reduce-scatter.15.cloned.1.call-done = bf16[8,4096]{1,0:T(8,128)(2,1)} async-done(((bf16[64,4096]{1,0:T(8,128)(2,1)}), bf16[8,4096]{1,0:T(8,128)(2,1)}) %reduce-scatter.15.cloned.1.call-update) | async-done | bytes 65552
  443.7 30.5 %all_gather.7 = bf16[64,1,64,64]{3,2,1,0:T(8,128)(2,1)S(1)} all-gather(bf16[8,1,64,64]{3,2,1,0:T(8,128)(2,1)S(1)} %bitcast.311), channel_id=1, replica_groups=mesh['gx'=32,'gy'=8] {'gy'}, dimensions={0}, use_global_device_ids=true | all-gather | bytes 589824 | tf_op jit(solution)/shard_map/all_gather | solution.py:88
  474.2 1.4 copy.155
  475.6 1.4 fusion.75
  477.1 5.2 %copy.147 = bf16[32,2,1,64,256]{4,1,0,3,2:T(2,128)(2,1)} copy(bf16[32,2,1,64,256]{4,1,3,2,0:T(2,128)(2,1)} %all-to-all-done.1) | data formatting | bytes 4194304 | tf_op jit(solution)/shard_map/all_to_all | solution.py:76
  482.3 4.1 reshape.451
  486.4 3.8 fusion.25
  490.2 10.8 %fusion.20 = bf16[1,64,64,256]{3,1,2,0:T(8,128)(2,1)S(1)} fusion(bf16[1,64,64,256]{3,1,2,0:T(8,128)(2,1)} %copy-done.1, bf16[64,64,256]{2,1,0:T(8,128)(2,1)} %fusion.25, bf16[2,256,64]{1,2,0:T(8,128)(2,1)S(1)} %copy-done.6, bf16[2,64,256]{2,1,0:T(8,128)(2,1)S(1)} %copy-done.8), kind=kOutput, calls=%fused_computation.23 | convolution fusion | flops 1114636288 | bytes 6356992 | tf_op jit(solution)/shard_map/hc,zhxy->zcxy/dot_general | solution.py:102
  501.0 2.5 copy.158
  (69 shorter events, 17.8 us)
Async XLA Ops:
  7.4 127.5 %reduce-scatter.9.cloned.1.call-start = ((), (), s32[]{:S(2)}) async-start(), calls=%async_computation.6 | async-start | bytes 2162688 | tf_op jit(solution)/shard_map/reduce_scatter | solution.py:57
  13.7 0.8 copy-start.4
  141.7 7.4 %copy-start = (bf16[1,64,64,256]{3,2,1,0:T(8,128)(2,1)S(1)}, bf16[1,64,64,256]{3,2,1,0:T(8,128)(2,1)}, u32[]{:S(2)}) copy-start(bf16[1,64,64,256]{3,2,1,0:T(8,128)(2,1)} %param.5) | copy-start | bytes 6291460
  141.7 90.4 %all-to-all-start = ((bf16[32,2,1,64,256]{4,1,3,2,0:T(2,128)(2,1)}), bf16[32,2,1,64,256]{4,1,3,2,0:T(2,128)(2,1)}, u32[]{:S(2)}, u32[]{:S(2)}) async-start(bf16[32,2,1,64,256]{4,1,3,2,0:T(2,128)(2,1)} %stack.64), calls=%async_computation.1 | async-start | bytes 4194304 | tf_op jit(solution)/shard_map/all_to_all | solution.py:76
  149.1 47.3 %reduce-scatter.13.cloned.1.call-start = ((), (), s32[]{:S(2)}) async-start(), calls=%async_computation.8 | async-start | bytes 589824
  150.3 2.4 copy-start.3
  152.6 226.0 %reduce-scatter.11.cloned.1.call-start = ((), (), s32[]{:S(2)}) async-start(), calls=%async_computation.7 | async-start | bytes 2162688 | tf_op jit(solution)/shard_map/reduce_scatter | solution.py:57
  241.4 3.8 copy-start.5
  241.4 3.8 copy-start.7
  257.6 135.1 %copy-start.1 = (bf16[1,64,64,256]{3,1,2,0:T(8,128)(2,1)}, bf16[1,64,64,256]{3,1,2,0:T(8,128)(2,1)S(1)}, u32[]{:S(2)}) copy-start(bf16[1,64,64,256]{3,1,2,0:T(8,128)(2,1)S(1)} %fusion.22) | copy-start | bytes 6291460
  261.9 116.7 %copy-start.2 = (bf16[1,2,64,64]{3,2,1,0:T(8,128)(2,1)S(1)}, bf16[1,2,64,64]{3,2,1,0:T(8,128)(2,1)}, u32[]{:S(2)}) copy-start(bf16[1,2,64,64]{3,2,1,0:T(8,128)(2,1)} %get-tuple-element.7) | copy-start | bytes 49156
  385.4 91.6 %all-to-all-start.1 = ((bf16[32,2,1,64,256]{4,1,3,2,0:T(2,128)(2,1)}), bf16[32,2,1,64,256]{4,1,3,2,0:T(2,128)(2,1)}, u32[]{:S(2)}, u32[]{:S(2)}) async-start(bf16[32,2,1,64,256]{4,1,3,2,0:T(2,128)(2,1)} %stack.72), calls=%async_computation.3 | async-start | bytes 4194304 | tf_op jit(solution)/shard_map/all_to_all | solution.py:76
  392.6 49.0 %reduce-scatter.15.cloned.1.call-start = ((), (), s32[]{:S(2)}) async-start(), calls=%async_computation.9 | async-start | bytes 589824
  486.4 3.8 copy-start.6
  486.4 3.8 copy-start.8
Sparse Core Ops, SparseCore 0:
  13.9 120.9 reduce-scatter.8
  262.1 116.4 reduce-scatter.10
Sparse Core Ops, SparseCore 1:
  152.7 43.6 reduce-scatter.12
  397.7 43.8 reduce-scatter.14
